TPU v7x, 32 devices: a whole 2x2x4 slice. The times are simulated.
32 devices in a mesh: groups: 2 (over y), context: 4 (over x, core), tensor: 4 (over z).
Axes of the slice: x: 2, y: 2, z: 4, core: 2. Of those that a mesh axis runs over, the one named last changes fastest.
Arguments:
- tokens: bfloat16 [4096, 4096], P(('groups', 'context', 'tensor')), parts along dimension 0, may hold values from -1000 to 1000
- norm_gain: bfloat16 [4096], replicated, may hold values from 0.099609375 to 1.8984375
- w_in: bfloat16 [4096, 3, 4096], P('context', None, 'tensor'), may hold values from -0.09375 to 0.09375
- short_filter: float32 [3, 3, 4096], P(None, None, 'tensor'), may hold values from -3.6 to 3.6
- medium_filter: float32 [128, 4096], P(None, 'tensor'), may hold values from -0.9 to 0.9
- decay: float32 [4096], P('tensor'), may hold values from 0.004 to 0.12
- w_out: bfloat16 [4096, 4096], P('context', 'tensor'), may hold values from -0.09375 to 0.09375
Outputs:
- mixer_out: bfloat16 [4096, 4096], P(('groups', 'context', 'tensor')), parts along dimension 0
There are 2 independent parts, one for each index of `groups`. A program takes and returns all parts, laid end to end along the dimension named above; an argument that names none is the same for every part. Nothing has to cross between parts.
All inputs are finite; a program needn't handle non-finite values.
Results may differ from a plain program's by a relative error of at most 0.01.
Values may be sent and summed in bfloat16 or wider, within the bound.
No kernel may reach another device: no remote copies, remote signals or barrier semaphores. Data moves between devices by JAX's collectives and lax.ppermute only.
A program may use at most 128 MiB of HBM per device.

v0:
```python
import jax
import jax.numpy as jnp
from jax import lax
from jax.sharding import PartitionSpec as P

norm_epsilon = 1e-06
lag_group = 8


def shifted_2(value, axis, steps):
    count = lax.axis_size(axis)
    first, last = (max(0, -steps), min(count, count - steps))
    return lax.ppermute(value, axis, [(source, source + steps) for source in range(first, last)])


def causal_short(extended, short_taps, out_count):
    tap_count = short_taps.shape[0]
    result = short_taps[0][None] * extended[tap_count - 1 : tap_count - 1 + out_count]
    for lag in range(1, tap_count):
        result = (
            result
            + short_taps[lag][None]
            * extended[tap_count - 1 - lag : tap_count - 1 - lag + out_count]
        )
    return result


def local(tokens, norm_gain, w_in, short_filter, medium_filter, decay, w_out):
    values = tokens.astype(jnp.float32)
    inverse_rms = lax.rsqrt(jnp.mean(values * values, axis=1, keepdims=True) + norm_epsilon)
    normed = (values * inverse_rms * norm_gain.astype(jnp.float32)[None, :]).astype(jnp.bfloat16)
    gathered = lax.all_gather(normed, "tensor", axis=0, tiled=True)
    slab_length = gathered.shape[0]
    channels = w_in.shape[2]
    shard_rows = lax.all_gather(w_in, "context", axis=0, tiled=True)
    row_count = shard_rows.shape[0]
    projection_acc = jnp.dot(
        gathered, shard_rows.reshape(row_count, 3 * channels), preferred_element_type=jnp.float32
    )
    projected = projection_acc.astype(jnp.bfloat16).reshape(slab_length, 3, channels)
    short_taps = short_filter.shape[0]
    medium_taps = medium_filter.shape[0]
    short_edge = shifted_2(projected[slab_length - (short_taps - 1) :], "context", 1)
    featured = causal_short(
        jnp.concatenate([short_edge, projected], axis=0).astype(jnp.float32),
        short_filter,
        slab_length,
    )
    query_feat = featured[:, 0]
    gated = (featured[:, 1] * featured[:, 2]).astype(jnp.bfloat16)
    gated_edge = shifted_2(gated[slab_length - (medium_taps - 1) :], "context", 1)
    gated_ext = jnp.concatenate([gated_edge, gated], axis=0)
    lag_index = jnp.arange(medium_taps, dtype=jnp.float32)
    filter_taps = (medium_filter * jnp.exp(-decay[None, :] * lag_index[:, None])).astype(
        jnp.bfloat16
    )

    def add_lags(turn, total):
        first_lag = turn * lag_group
        for offset in range(lag_group):
            lag = first_lag + offset
            shifted = lax.dynamic_slice_in_dim(gated_ext, medium_taps - 1 - lag, slab_length, 0)
            weights = lax.dynamic_slice_in_dim(filter_taps, lag, 1, 0)
            total = total + weights.astype(jnp.float32) * shifted.astype(jnp.float32)
        return total

    mixed = lax.fori_loop(
        0, medium_taps // lag_group, add_lags, jnp.zeros((slab_length, channels), jnp.float32)
    )
    combined = (query_feat * mixed).astype(jnp.bfloat16)
    out_full = lax.all_gather(w_out, "context", axis=0, tiled=True)
    return lax.psum_scatter(
        lax.dot_general(
            combined, out_full, (((1,), (1,)), ((), ())), preferred_element_type=jnp.float32
        ).astype(jnp.bfloat16),
        "tensor",
        scatter_dimension=0,
        tiled=True,
    )


def solution(mesh):
    in_specs = (
        P(("groups", "context", "tensor"), None),
        P(),
        P("context", None, "tensor"),
        P(None, None, "tensor"),
        P(None, "tensor"),
        P("tensor"),
        P("context", "tensor"),
    )
    out_specs = P(("groups", "context", "tensor"), None)
    return jax.shard_map(local, mesh=mesh, in_specs=in_specs, out_specs=out_specs, check_vma=False)
```

profile of v0, /device:TPU:0, one launch (start us, length us, event | category | flops | bytes accessed | tf_op | source)
XLA Modules:
  0.0 461.0 jit_solution(12642814142959749235)
XLA Ops:
  8.8 2.5 fusion.11
  11.4 8.6 %copy.10 = bf16[1024,3,1024]{0,2,1:T(8,128)(2,1)} copy(bf16[1024,3,1024]{2,0,1:T(8,128)(2,1)} %param.11) | data formatting | bytes 12582912 | tf_op args[2]
  21.9 73.0 %all-gather.4.cloned.1.call-done = bf16[512,4096]{1,0:T(8,128)(2,1)} async-done(((bf16[128,4096]{1,0:T(8,128)(2,1)}), bf16[512,4096]{1,0:T(8,128)(2,1)}) %all-gather.4.cloned.1.call-update) | async-done | bytes 4194320 | tf_op jit(solution)/shard_map/all_gather | solution.py:32
  94.9 154.9 %all-gather.6.cloned.1.call-done = bf16[4096,3,1024]{0,2,1:T(8,128)(2,1)} async-done(((bf16[1024,3,1024]{0,2,1:T(8,128)(2,1)}), bf16[4096,3,1024]{0,2,1:T(8,128)(2,1)}) %all-gather.6.cloned.1.call-update) | async-done | bytes 25165840 | tf_op jit(solution)/shard_map/all_gather | solution.py:35
  249.9 18.4 %convolution_convert_fusion.1 = bf16[512,3072]{1,0:T(8,128)(2,1)S(1)} fusion(bf16[512,4096]{1,0:T(8,128)(2,1)} %all-gather.4.cloned.1.call-done, bf16[4096,3072]{0,1:T(8,128)(2,1)} %bitcast.55), kind=kOutput, calls=%fused_computation.22 | convolution fusion | flops 12886474752 | bytes 32505856 | tf_op jit(solution)/shard_map/dot_general | solution.py:37
  268.4 2.1 collective-permute-start
  270.6 4.7 %copy.11 = bf16[512,3072]{0,1:T(8,128)(2,1)} copy(bf16[512,3072]{1,0:T(8,128)(2,1)} %copy-done.1) | data formatting | bytes 6291456 | tf_op jit(solution)/shard_map/convert_element_type | solution.py:40
  275.7 3.6 maximum_convert_fusion
  279.3 5.6 %fusion.7 = f32[512,3,1024]{0,2,1:T(8,128)S(1)} fusion(f32[514,3,1024]{0,2,1:T(8,128)S(1)} %maximum_convert_fusion, f32[3,1024]{1,0:T(4,128)S(1)} %get-tuple-element.193, f32[3,1024]{1,0:T(4,128)S(1)} %get-tuple-element.194, f32[3,1024]{1,0:T(4,128)S(1)} %get-tuple-element.192), kind=kLoop, calls=%fused_computation.17 | loop fusion | flops 7864320 | bytes 25202688 | tf_op jit(solution)/shard_map/add | solution.py:21
  285.4 2.1 collective-permute-start.1
  288.5 1.7 pad_maximum_fusion
  290.2 1.6 copy.13
  291.8 62.5 %while.17 = (s32[]{:T(128)}, f32[512,1024]{1,0:T(8,128)S(1)}, bf16[128,1024]{1,0:T(8,128)(2,1)}, bf16[639,1024]{1,0:T(8,128)(2,1)S(1)}, s32[]{:T(128)}, /*index=...) while((s32[]{:T(128)}, f32[512,1024]{1,0:T(8,128)S(1)}, ...), condition=%wide.region_2.0_spmd.clone, body=%wide.region_1.0_spmd.clone.sunk | while | flops 13115459 | bytes 12665847 | solution.py:67
  293.0 2.7 fusion.21
  296.9 2.7 fusion.21
  300.8 2.7 fusion.21
  304.7 2.7 fusion.21
  308.6 2.7 fusion.21
  312.5 2.7 fusion.21
  316.4 2.7 fusion.21
  320.3 2.7 fusion.21
  324.2 2.7 fusion.21
  328.1 2.7 fusion.21
  332.2 2.7 fusion.21
  336.1 2.7 fusion.21
  340.0 2.7 fusion.21
  343.9 2.7 fusion.21
  347.7 2.7 fusion.21
  351.6 2.7 fusion.21
  354.3 1.9 copy.14
  356.2 11.3 %convolution_convert_fusion = bf16[512,4096]{1,0:T(8,128)(2,1)} fusion(bf16[4096,1024]{1,0:T(8,128)(2,1)} %all-gather.8.cloned.1.call-done, f32[512,1024]{0,1:T(8,128)} %copy.14, f32[512,3,1024]{0,2,1:T(8,128)} %copy-done), kind=kOutput, calls=%fused_computation.21 | convolution fusion | flops 4298113024 | bytes 16777216 | tf_op jit(solution)/shard_map/dot_general | solution.py:73
  367.5 86.9 %reduce-scatter.2.cloned.1.call-done = bf16[128,4096]{1,0:T(8,128)(2,1)} async-done(((bf16[512,4096]{1,0:T(8,128)(2,1)}), bf16[128,4096]{1,0:T(8,128)(2,1)}) %reduce-scatter.2.cloned.1.call-update) | async-done | bytes 1048592 | tf_op jit(solution)/shard_map/reduce_scatter | solution.py:72
  (50 shorter events, 23.2 us)
Async XLA Ops:
  6.5 88.4 %all-gather.4.cloned.1.call-start = ((), (), s32[]{:S(2)}) async-start(), calls=%async_computation.1 | async-start | bytes 5242880 | tf_op jit(solution)/shard_map/all_gather | solution.py:32
  11.3 238.6 %all-gather.6.cloned.1.call-start = ((), (), s32[]{:S(2)}) async-start(), calls=%async_computation.2 | async-start | bytes 31457280 | tf_op jit(solution)/shard_map/all_gather | solution.py:35
  20.0 0.8 copy-start.4
  20.0 1.1 copy-start.2
  20.0 336.2 %all-gather.8.cloned.1.call-start = ((), (), s32[]{:S(2)}) async-start(), calls=%async_computation.3 | async-start | bytes 10485760 | tf_op jit(solution)/shard_map/all_gather | solution.py:71
  20.8 433.6 %reduce-scatter.2.cloned.1.call-start = ((), (), s32[]{:S(2)}) async-start(), calls=%async_computation.4 | async-start | bytes 5242880 | tf_op jit(solution)/shard_map/reduce_scatter | solution.py:72
  249.9 20.7 %copy-start.3 = (f32[3,3,1024]{2,1,0:T(4,128)S(1)}, f32[3,3,1024]{2,1,0:T(4,128)}, u32[]{:S(2)}) copy-start(f32[3,3,1024]{2,1,0:T(4,128)} %param.12) | copy-start | bytes 110596
  268.3 2.2 copy-start.1
  268.4 6.9 %collective-permute-start = (bf16[2,3,1024]{2,1,0:T(4,128)(2,1)S(1)}, bf16[2,3,1024]{2,1,0:T(4,128)(2,1)S(1)}, u32[]{:S(2)}, u32[]{:S(2)}) collective-permute-start(bf16[2,3,1024]{2,1,0:T(4,128)(2,1)S(1)} %slice.41), channel_id=1, source_target_pairs={{0,4},{4,8},{8,12},{1,5},{5,9},{9,13},{2,6},{6,10},{10,14},{3,7},{... | collective-permute-start | bytes 36872 | tf_op jit(solution)/shard_map/ppermute | solution.py:13
  284.9 3.6 copy-start
  285.4 3.1 collective-permute-start.1
Sparse Core Ops, SparseCore 0:
  11.4 83.4 all-gather.3
  96.5 153.3 all-gather.5
  251.4 58.2 all-gather.7
  367.6 86.7 reduce-scatter.1
where the time goes:
time: 463 us; the launch traced here: 461 us
  waiting for transfers between devices  316 us (68%)
  other arithmetic  77.4 us (17%)
  matrix products  29.7 us (6%)
  local copies, waits for them, and re-layouts  17.7 us (4%)
  between operations  13.3 us (3%)
    all_gather x1, waiting for transfers between devices, local(): shard_rows = lax.all_gather(w_in, 'context', axis=0, tiled=True)  155 us
    reduce_scatter x1, waiting for transfers between devices, local(): lax.psum_scatter(lax.dot_general(combined, out_full, (((1,), (1,)), ((),...  86.9 us
    all_gather x1, waiting for transfers between devices, local(): gathered = lax.all_gather(normed, 'tensor', axis=0, tiled=True)  73 us
    add x16, other arithmetic, add_lags(): total = total + weights.astype(jnp.float32) * shifted.astype(jnp.float32)  43.1 us
    dot_general x1, matrix products, local(): jnp.dot(gathered, shard_rows.reshape(row_count, 3 * channels), preferred_...  18.4 us
    mul x16, other arithmetic, add_lags(): total = total + weights.astype(jnp.float32) * shifted.astype(jnp.float32)  17.1 us
    dot_general x1, matrix products, local(): lax.dot_general(combined, out_full, (((1,), (1,)), ((), ())), preferred_e...  11.3 us
    unnamed x12, local copies, waits for them, and re-layouts  10.5 us
  transfers between devices with their start and end apart: 6, of which 4 were waited for; matrix products, arithmetic and copies ran while one was open for 24% of the time, Pallas kernels for 0%

commit v1 on v0

--- a/solution.py
+++ b/solution.py
@@ -5,6 +5,17 @@
 
 norm_epsilon = 1e-06
 lag_group = 8
+
+
+def around_the_ring(block, mesh_axis, d):
+    devices = lax.axis_size(mesh_axis)
+    right = [(i, (i + 1) % devices) for i in range(devices)]
+    parts = [block]
+    for far in range(1, devices):
+        parts = [lax.ppermute(parts[0], mesh_axis, right), *parts]
+    full = jnp.concatenate(parts, axis=d)
+    turn = (lax.axis_index(mesh_axis) + 1) * parts[-1].shape[d]
+    return jnp.roll(full, turn, axis=d)
 
 
 def shifted_2(value, axis, steps):
@@ -29,7 +40,7 @@
     values = tokens.astype(jnp.float32)
     inverse_rms = lax.rsqrt(jnp.mean(values * values, axis=1, keepdims=True) + norm_epsilon)
     normed = (values * inverse_rms * norm_gain.astype(jnp.float32)[None, :]).astype(jnp.bfloat16)
-    gathered = lax.all_gather(normed, "tensor", axis=0, tiled=True)
+    gathered = around_the_ring(normed, "tensor", 0)
     slab_length = gathered.shape[0]
     channels = w_in.shape[2]
     shard_rows = lax.all_gather(w_in, "context", axis=0, tiled=True)

time: 463 us -> 387 us (0.84)
  waiting for transfers between devices: 316 us -> 227 us
  local copies, waits for them, and re-layouts: 17.7 us -> 29 us
    all_gather x1, waiting for transfers between devices: 155 us -> 64.6 us  [local(): shard_rows = lax.all_gather(w_in, 'context', axis=0, tiled=True)]
    ppermute x0 -> x3, waiting for transfers between devices: none -> 74.7 us  [around_the_ring(): parts = [lax.ppermute(parts[0], mesh_axis, right), *parts]]
    all_gather x1 -> x0, waiting for transfers between devices: 73 us -> none  [local(): gathered = lax.all_gather(normed, 'tensor', axis=0, tiled=True)]
    unnamed x12 -> x20, local copies, waits for them, and re-layouts: 10.5 us -> 21.9 us
  transfers between devices with their start and end apart: 6 -> 8, of which waited for: 4 -> 6; matrix products, arithmetic and copies ran while one was open for 24% -> 29% of each run, Pallas kernels for 0% -> 0%
where the time goes in v1:
time: 387 us; the launch traced here: 385 us
  waiting for transfers between devices  227 us (59%)
  other arithmetic  76.8 us (20%)
  matrix products  29.7 us (8%)
  local copies, waits for them, and re-layouts  29 us (7%)
  between operations  13.3 us (3%)
  starting transfers between devices  7.49 us (2%)
    reduce_scatter x1, waiting for transfers between devices, local(): lax.psum_scatter(lax.dot_general(combined, out_full, (((1,), (1,)), ((),...  86.8 us
    ppermute x3, waiting for transfers between devices, around_the_ring(): parts = [lax.ppermute(parts[0], mesh_axis, right), *parts]  74.7 us
    all_gather x1, waiting for transfers between devices, local(): shard_rows = lax.all_gather(w_in, 'context', axis=0, tiled=True)  64.6 us
    add x16, other arithmetic, add_lags(): total = total + weights.astype(jnp.float32) * shifted.astype(jnp.float32)  43.1 us
    unnamed x20, local copies, waits for them, and re-layouts  21.9 us
    dot_general x1, matrix products, local(): jnp.dot(gathered, shard_rows.reshape(row_count, 3 * channels), preferred_...  18.4 us
    mul x16, other arithmetic, add_lags(): total = total + weights.astype(jnp.float32) * shifted.astype(jnp.float32)  16.9 us
    dot_general x1, matrix products, local(): lax.dot_general(combined, out_full, (((1,), (1,)), ((), ())), preferred_e...  11.3 us
  transfers between devices with their start and end apart: 8, of which 6 were waited for; matrix products, arithmetic and copies ran while one was open for 29% of the time, Pallas kernels for 0%

profile of v1, /device:TPU:0, one launch (start us, length us, event | category | flops | bytes accessed | tf_op | source)
XLA Modules:
  0.0 385.4 jit_solution(17510023904656719225)
XLA Ops:
  6.5 8.6 %copy.10 = bf16[1024,3,1024]{0,2,1:T(8,128)(2,1)} copy(bf16[1024,3,1024]{2,0,1:T(8,128)(2,1)} %param.11) | data formatting | bytes 12582912 | tf_op args[2]
  17.1 3.1 collective-permute-start
  20.1 25.2 %collective-permute-done = bf16[128,4096]{1,0:T(8,128)(2,1)S(1)} collective-permute-done((bf16[128,4096]{1,0:T(8,128)(2,1)S(1)}, bf16[128,4096]{1,0:T(8,128)(2,1)S(1)}, u32[]{:S(2)}, u32[]{:S(2)}) %collective-permute-start) | collective-permute-done | bytes 1048608 | tf_op jit(solution)/shard_map/ppermute | solution.py:15
  45.3 26.1 %collective-permute-done.1 = bf16[128,4096]{1,0:T(8,128)(2,1)S(1)} collective-permute-done((bf16[128,4096]{1,0:T(8,128)(2,1)S(1)}, bf16[128,4096]{1,0:T(8,128)(2,1)S(1)}, u32[]{:S(2)}, u32[]{:S(2)}) %collective-permute-start.1) | collective-permute-done | bytes 1048608 | tf_op jit(solution)/shard_map/ppermute | solution.py:15
  73.4 23.4 %collective-permute-done.2 = bf16[128,4096]{1,0:T(8,128)(2,1)} collective-permute-done((bf16[128,4096]{1,0:T(8,128)(2,1)S(1)}, bf16[128,4096]{1,0:T(8,128)(2,1)}, u32[]{:S(2)}, u32[]{:S(2)}) %collective-permute-start.2) | collective-permute-done | bytes 1048608 | tf_op jit(solution)/shard_map/ppermute | solution.py:15
  96.8 2.3 constant_dynamic-update-slice_fusion.7
  102.5 2.3 constant_dynamic-update-slice_fusion.3
  108.3 64.6 %all-gather.3.cloned.1.call-done = bf16[4096,3,1024]{0,2,1:T(8,128)(2,1)} async-done(((bf16[1024,3,1024]{0,2,1:T(8,128)(2,1)}), bf16[4096,3,1024]{0,2,1:T(8,128)(2,1)}) %all-gather.3.cloned.1.call-update) | async-done | bytes 25165840 | tf_op jit(solution)/shard_map/all_gather | solution.py:46
  172.9 18.4 %convolution_convert_fusion.1 = bf16[512,3072]{1,0:T(8,128)(2,1)S(1)} fusion(bf16[4096,3072]{0,1:T(8,128)(2,1)} %bitcast.54, bf16[1024,4096]{1,0:T(8,128)(2,1)} %constant_dynamic-update-slice_fusion, s32[]{:T(128)S(6)} %select_n.190), kind=kOutput, calls=%fused_computation.22 | convolution fusion | flops 12886474752 | bytes 32505860 | tf_op jit(solution)/shard_map/dot_general | solution.py:48
  195.2 4.7 %copy.11 = bf16[512,3072]{0,1:T(8,128)(2,1)} copy(bf16[512,3072]{1,0:T(8,128)(2,1)} %copy-done.2) | data formatting | bytes 6291456 | tf_op jit(solution)/shard_map/convert_element_type | solution.py:51
  200.3 3.6 maximum_convert_fusion
  203.9 5.6 %fusion.7 = f32[512,3,1024]{0,2,1:T(8,128)S(1)} fusion(f32[514,3,1024]{0,2,1:T(8,128)S(1)} %maximum_convert_fusion, f32[3,1024]{1,0:T(4,128)S(1)} %get-tuple-element.193, f32[3,1024]{1,0:T(4,128)S(1)} %get-tuple-element.194, f32[3,1024]{1,0:T(4,128)S(1)} %get-tuple-element.192), kind=kLoop, calls=%fused_computation.17 | loop fusion | flops 7864320 | bytes 25202688 | tf_op jit(solution)/shard_map/add | solution.py:32
  210.0 2.2 collective-permute-start.4
  216.6 62.3 %while.17 = (s32[]{:T(128)}, f32[512,1024]{1,0:T(8,128)S(1)}, bf16[128,1024]{1,0:T(8,128)(2,1)}, bf16[639,1024]{1,0:T(8,128)(2,1)S(1)}, s32[]{:T(128)}, /*index=...) while((s32[]{:T(128)}, f32[512,1024]{1,0:T(8,128)S(1)}, ...), condition=%wide.region_2.3_spmd.clone, body=%wide.region_1.2_spmd.clone.sunk | while | flops 13115459 | bytes 12665847 | solution.py:78
  217.8 2.7 fusion.22
  221.7 2.7 fusion.22
  225.6 2.7 fusion.22
  229.4 2.7 fusion.22
  233.3 2.7 fusion.22
  237.2 2.7 fusion.22
  241.1 2.7 fusion.22
  245.0 2.7 fusion.22
  248.9 2.7 fusion.22
  252.8 2.7 fusion.22
  256.7 2.7 fusion.22
  260.6 2.7 fusion.22
  264.5 2.7 fusion.22
  268.4 2.7 fusion.22
  272.3 2.7 fusion.22
  276.2 2.7 fusion.22
  280.7 11.3 %convolution_convert_fusion = bf16[512,4096]{1,0:T(8,128)(2,1)} fusion(bf16[4096,1024]{1,0:T(8,128)(2,1)} %all-gather.5.cloned.1.call-done, f32[512,1024]{0,1:T(8,128)} %copy.14, f32[512,3,1024]{0,2,1:T(8,128)} %copy-done), kind=kOutput, calls=%fused_computation.21 | convolution fusion | flops 4298113024 | bytes 16777216 | tf_op jit(solution)/shard_map/dot_general | solution.py:84
  292.0 86.8 %reduce-scatter.2.cloned.1.call-done = bf16[128,4096]{1,0:T(8,128)(2,1)} async-done(((bf16[512,4096]{1,0:T(8,128)(2,1)}), bf16[128,4096]{1,0:T(8,128)(2,1)}) %reduce-scatter.2.cloned.1.call-update) | async-done | bytes 1048592 | tf_op jit(solution)/shard_map/reduce_scatter | solution.py:83
  (63 shorter events, 38.5 us)
Async XLA Ops:
  6.5 166.3 %all-gather.3.cloned.1.call-start = ((), (), s32[]{:S(2)}) async-start(), calls=%async_computation.1 | async-start | bytes 31457280 | tf_op jit(solution)/shard_map/all_gather | solution.py:46
  15.2 0.7 copy-start.4
  15.2 1.2 copy-start.1
  15.2 265.5 %all-gather.5.cloned.1.call-start = ((), (), s32[]{:S(2)}) async-start(), calls=%async_computation.2 | async-start | bytes 10485760 | tf_op jit(solution)/shard_map/all_gather | solution.py:82
  16.7 54.8 %copy-start.5 = (f32[1024]{0:T(1024)S(1)}, f32[1024]{0:T(1024)}, u32[]{:S(2)}) copy-start(f32[1024]{0:T(1024)} %param.14) | copy-start | bytes 12292
  17.1 28.3 %collective-permute-start = (bf16[128,4096]{1,0:T(8,128)(2,1)S(1)}, bf16[128,4096]{1,0:T(8,128)(2,1)S(1)}, u32[]{:S(2)}, u32[]{:S(2)}) collective-permute-start(bf16[128,4096]{1,0:T(8,128)(2,1)S(1)} %fusion.12), channel_id=1, source_target_pairs={{0,1},{1,2},{2,3},{3,0},{4,5},{5,6},{6,7},{7,4},{8,9},{9,10},{10,1... | collective-permute-start | bytes 3145736 | tf_op jit(solution)/shard_map/ppermute | solution.py:15
  45.3 26.1 %collective-permute-start.1 = (bf16[128,4096]{1,0:T(8,128)(2,1)S(1)}, bf16[128,4096]{1,0:T(8,128)(2,1)S(1)}, u32[]{:S(2)}, u32[]{:S(2)}) collective-permute-start(bf16[128,4096]{1,0:T(8,128)(2,1)S(1)} %collective-permute-done), channel_id=1, source_target_pairs={{0,1},{1,2},{2,3},{3,0},{4,5},{5,6},{6,7},{7,4},{8,9},{9,10},{10,1... | collective-permute-start | bytes 3145736 | tf_op jit(solution)/shard_map/ppermute | solution.py:15
  71.5 25.3 %collective-permute-start.2 = (bf16[128,4096]{1,0:T(8,128)(2,1)S(1)}, bf16[128,4096]{1,0:T(8,128)(2,1)}, u32[]{:S(2)}, u32[]{:S(2)}) collective-permute-start(bf16[128,4096]{1,0:T(8,128)(2,1)S(1)} %collective-permute-done.1), channel_id=1, source_target_pairs={{0,1},{1,2},{2,3},{3,0},{4,5},{5,6},{6,7},{7,4},{8,9},{9,10},{10,1... | collective-permute-start | bytes 3145736 | tf_op jit(solution)/shard_map/ppermute | solution.py:15
  71.5 307.4 %reduce-scatter.2.cloned.1.call-start = ((), (), s32[]{:S(2)}) async-start(), calls=%async_computation.3 | async-start | bytes 5242880 | tf_op jit(solution)/shard_map/reduce_scatter | solution.py:83
  172.9 22.3 %copy-start.3 = (f32[3,3,1024]{2,1,0:T(4,128)S(1)}, f32[3,3,1024]{2,1,0:T(4,128)}, u32[]{:S(2)}) copy-start(f32[3,3,1024]{2,1,0:T(4,128)} %param.12) | copy-start | bytes 110596
  191.3 1.7 copy-start.2
  193.0 6.9 %collective-permute-start.3 = (bf16[2,3,1024]{2,1,0:T(4,128)(2,1)S(1)}, bf16[2,3,1024]{2,1,0:T(4,128)(2,1)S(1)}, u32[]{:S(2)}, u32[]{:S(2)}) collective-permute-start(bf16[2,3,1024]{2,1,0:T(4,128)(2,1)S(1)} %slice.41), channel_id=1, source_target_pairs={{0,4},{4,8},{8,12},{1,5},{5,9},{9,13},{2,6},{6,10},{10,14},{3,7},{... | collective-permute-start | bytes 36872 | tf_op jit(solution)/shard_map/ppermute | solution.py:24
  209.5 3.7 copy-start
  210.0 3.1 collective-permute-start.4
Sparse Core Ops, SparseCore 0:
  15.3 157.4 all-gather.2
  174.4 58.2 all-gather.4
  292.2 86.6 reduce-scatter.1
